TPU v7x, 256 devices: a whole 4x4x8 slice. The times are simulated.
256 devices in a mesh: shot: 32 (over z, x_hi, core), dom: 8 (over y, x_lo).
Axes of the slice: x: 4 (x_hi: 2, x_lo: 2; x = x_hi * 2 + x_lo), y: 4, z: 8, core: 2. Of those that a mesh axis runs over, the one named last changes fastest.
Arguments:
- velocity: float32 [64, 128, 256], P('dom', 'shot'), may hold values from 0.15 to 0.4
- epsilon: float32 [64, 128, 256], P('dom', 'shot'), may hold values from 0.05 to 0.3
- forward_state: float32 [32, 4, 64, 128, 256], P('shot', None, 'dom'), may hold values from -1.2 to 1.2
- adjoint_state: float32 [32, 4, 64, 128, 256], P('shot', None, 'dom'), may hold values from -1.2 to 1.2
- source_cell: int32 [32], P('shot'), may hold values from 0 to 2097151
- wavelet: float32 [32, 3], P('shot'), may hold values from -6 to 6
- receiver_cells: int32 [32, 256], P('shot'), may hold values from 0 to 2097151
- residuals: float32 [32, 4, 256], P('shot'), may hold values from -6 to 6
Outputs:
- velocity_grad: float32 [64, 128, 256], P('dom', 'shot')
- epsilon_grad: float32 [64, 128, 256], P('dom', 'shot')
Inputs may be any that keep to these rules, and one draw needn't show every extreme that they name: `source_cell`: flat grid cell index (z * 128 + x) * 256 + y of each shot's source. `receiver_cells`: flat grid cell indices (z * 128 + x) * 256 + y of each shot's receivers; two receivers may share a cell.
All inputs are finite; a program needn't handle non-finite values.
Results may differ from a plain program's by a relative error of at most 0.00002.
Values sent between devices are 32-bit elements; how exact they have to be, the bound alone decides.
No kernel may reach another device: no remote copies, remote signals or barrier semaphores. Data moves between devices by JAX's collectives and lax.ppermute only.
A program may use at most 128 MiB of HBM per device.

v0:
```python
import jax
import jax.numpy as jnp
from jax import lax
from jax.sharding import PartitionSpec as P

STEPS = 4


def with_halo(cells, sides, width):
    for axis, dim in sides:
        count = lax.axis_size(axis)
        ends = count - 1
        head = lax.slice_in_dim(cells, 0, width, axis=dim)
        tail = lax.slice_in_dim(cells, cells.shape[dim] - width, cells.shape[dim], axis=dim)
        cells = jnp.concatenate(
            [
                lax.ppermute(tail, axis, [(i, (i + 1) % count) for i in range(ends)]),
                cells,
                lax.ppermute(head, axis, [((i + 1) % count, i) for i in range(ends)]),
            ],
            axis=dim,
        )
    return cells


def stencil(padded, axis, size):

    def part(offset):
        return lax.slice_in_dim(padded, offset, offset + size, axis=axis)

    return 4.0 / 3.0 * (part(1) + part(3)) - 1.0 / 12.0 * (part(0) + part(4)) - 2.5 * part(2)


def second_diff(field, axis):
    widths = [(0, 0), (0, 0), (0, 0)]
    widths[axis] = (2, 2)
    return stencil(jnp.pad(field, widths), axis, field.shape[axis])


def lateral(field):
    return second_diff(field, 1) + second_diff(field, 2)


def forward_vertical(field):
    padded = with_halo(field, (("dom", 0),), 2)
    return stencil(padded, 0, field.shape[0])


def adjoint_vertical(field):
    padded = with_halo(field, (("dom", 0),), 2)
    return stencil(padded, 0, field.shape[0])


def sum_shots(first_term, second_term, share_rows):
    whole_one, whole_two = lax.psum((first_term, second_term), "shot")
    offset = lax.axis_index("shot") * share_rows
    return (
        lax.dynamic_slice_in_dim(whole_one, offset, share_rows, 1),
        lax.dynamic_slice_in_dim(whole_two, offset, share_rows, 1),
    )


def on_device(
    velocity, epsilon, forward_state, adjoint_state, source_cell, wavelet, receiver_cells, residuals
):
    vel_slab, eps_slab = (
        lax.all_gather(velocity, "shot", axis=1, tiled=True),
        lax.all_gather(epsilon, "shot", axis=1, tiled=True),
    )
    stiffness = vel_slab * vel_slab
    stretch = 1.0 + 2.0 * eps_slab
    slab_depth, slab_width, slab_length = stiffness.shape
    plane_size = slab_width * slab_length
    first_layer = lax.axis_index("dom") * slab_depth

    def inject(field, cell_ids, amounts):
        layer_ids = cell_ids // plane_size - first_layer
        inside = (layer_ids >= 0) & (layer_ids < slab_depth)
        layer_ids = jnp.where(inside, layer_ids, 0)
        within = cell_ids % plane_size
        flattened = (
            field.reshape(-1)
            .at[layer_ids * plane_size + within]
            .add(jnp.where(inside, amounts, 0.0))
        )
        return flattened.reshape(field.shape)

    source = source_cell[0]
    receivers = receiver_cells[0]
    pressure_old, pressure_now = (forward_state[0, 0], forward_state[0, 1])
    support_old, support_now = (forward_state[0, 2], forward_state[0, 3])
    flat_terms = []
    depth_terms = []
    for moment in range(STEPS):
        flat_term = lateral(pressure_now)
        depth_term = forward_vertical(support_now)
        flat_terms.append(flat_term)
        depth_terms.append(depth_term)
        if moment + 1 < STEPS:
            pressure_new = (
                2.0 * pressure_now - pressure_old + stiffness * (stretch * flat_term + depth_term)
            )
            support_new = 2.0 * support_now - support_old + stiffness * (flat_term + depth_term)
            pressure_new = inject(pressure_new, source, wavelet[0, moment])
            support_new = inject(support_new, source, wavelet[0, moment])
            pressure_old, pressure_now = (pressure_now, pressure_new)
            support_old, support_now = (support_now, support_new)
    back_old, back_now = (adjoint_state[0, 0], adjoint_state[0, 1])
    side_old, side_now = (adjoint_state[0, 2], adjoint_state[0, 3])
    image_one = jnp.zeros_like(stiffness)
    image_two = jnp.zeros_like(stiffness)
    for moment in reversed(range(STEPS)):
        back_new = 2.0 * back_now - back_old + lateral(stiffness * (stretch * back_now + side_now))
        back_new = inject(back_new, receivers, residuals[0, moment])
        side_new = 2.0 * side_now - side_old + adjoint_vertical(stiffness * (back_now + side_now))
        image_one = image_one + back_new * flat_terms[moment]
        image_two = (
            image_two
            + back_new * depth_terms[moment]
            + side_new * (flat_terms[moment] + depth_terms[moment])
        )
        back_old, back_now = (back_now, back_new)
        side_old, side_now = (side_now, side_new)
    share_rows = velocity.shape[1]
    vel_term = 2.0 * vel_slab * (stretch * image_one + image_two)
    eps_term = 2.0 * stiffness * image_one
    velocity_grad, epsilon_grad = sum_shots(vel_term, eps_term, share_rows)
    return (velocity_grad, epsilon_grad)


def solution(mesh):
    placed = (
        P("dom", "shot", None),
        P("dom", "shot", None),
        P("shot", None, "dom", None, None),
        P("shot", None, "dom", None, None),
        P("shot"),
        P("shot", None),
        P("shot", None),
        P("shot", None, None),
    )
    return jax.shard_map(
        on_device,
        mesh=mesh,
        in_specs=placed,
        out_specs=(P("dom", "shot", None), P("dom", "shot", None)),
        check_vma=False,
    )
```

profile of v0, /device:TPU:1, one launch (start us, length us, event | category | flops | bytes accessed | tf_op | source)
XLA Modules:
  0.0 653.6 jit_solution(7060213678199251076)
XLA Ops:
  11.2 3.9 collective-permute-start
  18.3 1.7 slice_bitcast_fusion
  20.1 7.6 %collective-permute-done.1 = f32[2,128,256]{2,1,0:T(8,128)S(1)} collective-permute-done((f32[2,128,256]{2,1,0:T(8,128)S(1)}, f32[2,128,256]{2,1,0:T(8,128)S(1)}, u32[]{:S(2)}, u32[]{:S(2)}) %collective-permute-start.1) | collective-permute-done | bytes 262176 | tf_op jit(solution)/shard_map/ppermute | solution.py:19
  27.7 65.5 %all-gather.3.cloned.1.call-done = f32[8,128,256]{2,0,1:T(8,128)} async-done(((f32[8,4,256]{2,0,1:T(8,128)}), f32[8,128,256]{2,0,1:T(8,128)}) %all-gather.3.cloned.1.call-update) | async-done | bytes 1048592 | tf_op jit(solution)/shard_map/all_gather | solution.py:67
  93.2 78.1 %all-gather.5.cloned.1.call-done = f32[8,128,256]{2,0,1:T(8,128)} async-done(((f32[8,4,256]{2,0,1:T(8,128)}), f32[8,128,256]{2,0,1:T(8,128)}) %all-gather.5.cloned.1.call-update) | async-done | bytes 1048592 | tf_op jit(solution)/shard_map/all_gather | solution.py:68
  171.3 5.2 fusion.121
  179.5 2.9 collective-permute-start.2
  183.3 1.8 copy.31
  189.9 6.9 %collective-permute-done.3 = f32[2,128,256]{2,1,0:T(8,128)S(1)} collective-permute-done((f32[2,128,256]{2,1,0:T(8,128)}, f32[2,128,256]{2,1,0:T(8,128)S(1)}, u32[]{:S(2)}, u32[]{:S(2)}) %collective-permute-start.3) | collective-permute-done | bytes 262176 | tf_op jit(solution)/shard_map/ppermute | solution.py:19
  196.8 4.2 multiply_add_fusion.4
  201.0 2.7 multiply_add_fusion.3
  206.3 1.7 slice.619
  208.1 4.9 collective-permute-start.4
  213.6 2.6 reshape.371
  216.2 2.7 copy.33
  220.5 2.6 reshape.369
  226.2 1.6 constant_dynamic-update-slice_fusion.4
  227.7 4.4 collective-permute-done.5
  232.2 2.9 multiply_add_fusion
  237.5 1.7 slice.682
  239.2 3.8 collective-permute-start.12
  243.1 5.0 fusion.123
  249.9 2.8 collective-permute-start.6
  255.1 1.6 copy.30
  256.7 4.2 scatter_fusion
  261.0 1.5 reshape.360
  262.7 5.0 add_multiply_fusion.5
  267.8 4.0 add_multiply_fusion.4
  273.7 4.5 collective-permute-start.8
  282.8 1.8 copy.35
  286.1 2.8 copy.36
  288.8 4.3 scatter_fusion.1
  293.2 1.5 reshape.376
  294.7 1.7 constant_dynamic-update-slice_fusion.9
  296.4 4.9 add_multiply_fusion.2
  302.2 4.6 collective-permute-start.10
  310.5 1.5 copy.37
  312.0 4.1 scatter_fusion.2
  316.1 2.5 reshape.378
  318.7 6.1 add_multiply_fusion.1
  327.4 4.3 scatter_fusion.3
  331.7 2.5 reshape.380
  334.3 9.8 %multiply_multiply_fusion = (f32[8,128,256]{2,1,0:T(8,128)}, f32[8,128,256]{2,1,0:T(8,128)}, f32[8,128,256]{2,1,0:T(8,128)}) fusion(f32[8,128,256]{2,1,0:T(8,128)} %reshape.380, f32[8,128,256]{2,1,0:T(8,128)} %copy-done.13, f32[8,128,256]{2,1,0:T(8,128)} %reshape.378, f32[8,128,256]{2,1,0:T(8,128)} %copy-done.15, f32[8,128,256]{2,1,0:T(8,128)S(1)} %reshape.376, ...), kind=kLoop, calls=%fused_computation.209 | loop fusion | flops 6815744 | bytes 13631488 | tf_op jit(solution)/shard_map/mul | solution.py:126
  345.3 4.9 collective-permute-start.14
  350.2 1.6 collective-permute-start.15
  353.9 5.5 collective-permute-done.15
  359.5 7.9 %fusion.9 = f32[8,128,256]{2,1,0:T(8,128)} fusion(f32[8,128,256]{2,1,0:T(8,128)} %get-tuple-element.104, f32[2,128,256]{2,1,0:T(8,128)S(1)} %collective-permute-done.15, f32[2,128,256]{2,1,0:T(8,128)S(1)} %collective-permute-done.14, f32[8,128,256]{2,1,0:T(8,128)S(1)} %copy-done.11, f32[8,128,256]{2,1,0:T(8,128)} %get-tuple-element.92, ...), kind=kLoop, calls=%fused_computation.65 | loop fusion | flops 13893632 | bytes 24641536 | tf_op jit(solution)/shard_map/mul | solution.py:125
  367.4 277.9 %all-reduce.19.cloned.1.call-done = (f32[8,128,256]{2,1,0:T(8,128)}, f32[8,128,256]{2,1,0:T(8,128)}) async-done(((f32[8,128,256]{2,1,0:T(8,128)}, f32[8,128,256]{2,1,0:T(8,128)}), (f32[8,128,256]{2,1,0:T(8,128)}, f32[8,128,256]{2,1,0:T(8,128)})) %all-reduce.19.cloned.1.call-update) | async-done | bytes 2097168 | tf_op jit(solution)/shard_map/psum | solution.py:55
  (141 shorter events, 48.1 us)
Async XLA Ops:
  7.2 10.0 %copy-start.32 = (f32[1,3]{1,0:T(1,128)S(1)}, f32[1,3]{1,0:T(1,128)}, u32[]{:S(2)}) copy-start(f32[1,3]{1,0:T(1,128)} %param.25) | copy-start | bytes 40
  7.2 86.1 %all-gather.3.cloned.1.call-start = ((), (), s32[]{:S(2)}) async-start(), calls=%async_computation | async-start | bytes 1081344 | tf_op jit(solution)/shard_map/all_gather | solution.py:67
  8.6 162.7 %all-gather.5.cloned.1.call-start = ((), (), s32[]{:S(2)}) async-start(), calls=%async_computation.1 | async-start | bytes 1081344 | tf_op jit(solution)/shard_map/all_gather | solution.py:68
  10.1 635.2 %all-reduce.19.cloned.1.call-start = ((), (), s32[]{:S(2)}) async-start(), calls=%async_computation.2 | async-start | bytes 4194304 | tf_op jit(solution)/shard_map/psum | solution.py:55
  11.2 8.9 %collective-permute-start = (f32[2,128,256]{2,1,0:T(8,128)S(1)}, f32[2,128,256]{2,1,0:T(8,128)S(1)}, u32[]{:S(2)}, u32[]{:S(2)}) collective-permute-start(f32[2,128,256]{2,1,0:T(8,128)S(1)} %get-tuple-element.99), channel_id=1, source_target_pairs={{0,1},{1,2},{2,3},{3,4},{4,5},{5,6},{6,7},{8,9},{9,10},{10,11},{11... | collective-permute-start | bytes 786440 | tf_op jit(solution)/shard_map/ppermute | solution.py:17
  15.2 12.6 %collective-permute-start.1 = (f32[2,128,256]{2,1,0:T(8,128)S(1)}, f32[2,128,256]{2,1,0:T(8,128)S(1)}, u32[]{:S(2)}, u32[]{:S(2)}) collective-permute-start(f32[2,128,256]{2,1,0:T(8,128)S(1)} %get-tuple-element.100), channel_id=1, source_target_pairs={{1,0},{2,1},{3,2},{4,3},{5,4},{6,5},{7,6},{9,8},{10,9},{11,10},{12... | collective-permute-start | bytes 786440 | tf_op jit(solution)/shard_map/ppermute | solution.py:19
  27.7 143.6 %copy-start.31 = (f32[2,128,256]{2,1,0:T(8,128)}, f32[2,128,256]{2,1,0:T(8,128)S(1)}, u32[]{:S(2)}) copy-start(f32[2,128,256]{2,1,0:T(8,128)S(1)} %collective-permute-done.1) | copy-start | bytes 786436
  171.3 5.2 copy-start
  171.3 5.3 copy-start.9
  176.6 1.3 copy-start.20
  178.4 3.9 copy-start.33
  178.4 4.6 copy-start.34
  179.5 9.2 %collective-permute-start.2 = (f32[2,128,256]{2,1,0:T(8,128)}, f32[2,128,256]{2,1,0:T(8,128)}, u32[]{:S(2)}, u32[]{:S(2)}) collective-permute-start(f32[2,128,256]{2,1,0:T(8,128)} %slice.602), channel_id=1, source_target_pairs={{0,1},{1,2},{2,3},{3,4},{4,5},{5,6},{6,7},{8,9},{9,10},{10,11},{11... | collective-permute-start | bytes 786440 | tf_op jit(solution)/shard_map/ppermute | solution.py:17
  187.4 9.4 %collective-permute-start.3 = (f32[2,128,256]{2,1,0:T(8,128)}, f32[2,128,256]{2,1,0:T(8,128)S(1)}, u32[]{:S(2)}, u32[]{:S(2)}) collective-permute-start(f32[2,128,256]{2,1,0:T(8,128)} %slice.605), channel_id=1, source_target_pairs={{1,0},{2,1},{3,2},{4,3},{5,4},{6,5},{7,6},{9,8},{10,9},{11,10},{12... | collective-permute-start | bytes 786440 | tf_op jit(solution)/shard_map/ppermute | solution.py:19
  189.7 7.1 %copy-start.1 = (f32[8,128,256]{2,0,1:T(8,128)S(1)}, f32[8,128,256]{2,0,1:T(8,128)}, u32[]{:S(2)}) copy-start(f32[8,128,256]{2,0,1:T(8,128)} %all-gather.5.cloned.1.call-done) | copy-start | bytes 3145732
  189.7 7.1 %copy-start.22 = (f32[8,128,256]{2,1,0:T(8,128)S(1)}, f32[8,128,256]{2,1,0:T(8,128)}, u32[]{:S(2)}) copy-start(f32[8,128,256]{2,1,0:T(8,128)} %reshape.364) | copy-start | bytes 3145732
  201.0 2.7 copy-start.15
  201.0 2.7 copy-start.21
  208.1 17.1 %collective-permute-start.4 = (f32[2,128,256]{2,1,0:T(8,128)}, f32[2,128,256]{2,1,0:T(8,128)}, u32[]{:S(2)}, u32[]{:S(2)}) collective-permute-start(f32[2,128,256]{2,1,0:T(8,128)} %slice.619), channel_id=1, source_target_pairs={{0,1},{1,2},{2,3},{3,4},{4,5},{5,6},{6,7},{8,9},{9,10},{10,11},{11... | collective-permute-start | bytes 786440 | tf_op jit(solution)/shard_map/ppermute | solution.py:17
  223.9 8.2 %collective-permute-start.5 = (f32[2,128,256]{2,1,0:T(8,128)}, f32[2,128,256]{2,1,0:T(8,128)S(1)}, u32[]{:S(2)}, u32[]{:S(2)}) collective-permute-start(f32[2,128,256]{2,1,0:T(8,128)} %slice.622), channel_id=1, source_target_pairs={{1,0},{2,1},{3,2},{4,3},{5,4},{6,5},{7,6},{9,8},{10,9},{11,10},{12... | collective-permute-start | bytes 786440 | tf_op jit(solution)/shard_map/ppermute | solution.py:19
  226.1 6.0 copy-start.23
  226.1 6.0 copy-start.24
  235.6 7.5 %copy-start.17 = (f32[8,128,256]{2,1,0:T(8,128)S(1)}, f32[8,128,256]{2,1,0:T(8,128)}, u32[]{:S(2)}) copy-start(f32[8,128,256]{2,1,0:T(8,128)} %get-tuple-element.81) | copy-start | bytes 3145732
  239.2 55.5 %collective-permute-start.12 = (f32[2,128,256]{2,1,0:T(8,128)}, f32[2,128,256]{2,1,0:T(8,128)}, u32[]{:S(2)}, u32[]{:S(2)}) collective-permute-start(f32[2,128,256]{2,1,0:T(8,128)} %slice.682), channel_id=1, source_target_pairs={{0,1},{1,2},{2,3},{3,4},{4,5},{5,6},{6,7},{8,9},{9,10},{10,11},{11... | collective-permute-start | bytes 786440 | tf_op jit(solution)/shard_map/ppermute | solution.py:17
  243.1 10.9 %copy-start.12 = (f32[1,4,8,128,256]{4,3,2,1,0:T(8,128)S(1)}, f32[1,4,8,128,256]{4,3,2,1,0:T(8,128)}, u32[]{:S(2)}) copy-start(f32[1,4,8,128,256]{4,3,2,1,0:T(8,128)} %param.23) | copy-start | bytes 12582916
  249.9 12.7 %collective-permute-start.6 = (f32[2,128,256]{2,1,0:T(8,128)}, f32[2,128,256]{2,1,0:T(8,128)}, u32[]{:S(2)}, u32[]{:S(2)}) collective-permute-start(f32[2,128,256]{2,1,0:T(8,128)} %get-tuple-element.125), channel_id=1, source_target_pairs={{0,1},{1,2},{2,3},{3,4},{4,5},{5,6},{6,7},{8,9},{9,10},{10,11},{11... | collective-permute-start | bytes 786440 | tf_op jit(solution)/shard_map/ppermute | solution.py:17
  252.7 10.1 %collective-permute-start.7 = (f32[2,128,256]{2,1,0:T(8,128)}, f32[2,128,256]{2,1,0:T(8,128)}, u32[]{:S(2)}, u32[]{:S(2)}) collective-permute-start(f32[2,128,256]{2,1,0:T(8,128)} %get-tuple-element.126), channel_id=1, source_target_pairs={{1,0},{2,1},{3,2},{4,3},{5,4},{6,5},{7,6},{9,8},{10,9},{11,10},{12... | collective-permute-start | bytes 786440 | tf_op jit(solution)/shard_map/ppermute | solution.py:19
  262.5 5.3 copy-start.2
  267.8 4.0 copy-start.5
  271.8 7.7 %copy-start.27 = (f32[262144]{0:T(1024)S(1)}, f32[262144]{0:T(1024)}, u32[]{:S(2)}) copy-start(f32[262144]{0:T(1024)} %copy-done.26) | copy-start | bytes 3145732
  273.7 22.7 %collective-permute-start.8 = (f32[2,128,256]{2,1,0:T(8,128)}, f32[2,128,256]{2,1,0:T(8,128)}, u32[]{:S(2)}, u32[]{:S(2)}) collective-permute-start(f32[2,128,256]{2,1,0:T(8,128)} %get-tuple-element.121), channel_id=1, source_target_pairs={{0,1},{1,2},{2,3},{3,4},{4,5},{5,6},{6,7},{8,9},{9,10},{10,11},{11... | collective-permute-start | bytes 786440 | tf_op jit(solution)/shard_map/ppermute | solution.py:17
  278.2 18.2 %collective-permute-start.9 = (f32[2,128,256]{2,1,0:T(8,128)}, f32[2,128,256]{2,1,0:T(8,128)}, u32[]{:S(2)}, u32[]{:S(2)}) collective-permute-start(f32[2,128,256]{2,1,0:T(8,128)} %get-tuple-element.122), channel_id=1, source_target_pairs={{1,0},{2,1},{3,2},{4,3},{5,4},{6,5},{7,6},{9,8},{10,9},{11,10},{12... | collective-permute-start | bytes 786440 | tf_op jit(solution)/shard_map/ppermute | solution.py:19
  281.5 71.4 %collective-permute-start.13 = (f32[2,128,256]{2,1,0:T(8,128)}, f32[2,128,256]{2,1,0:T(8,128)}, u32[]{:S(2)}, u32[]{:S(2)}) collective-permute-start(f32[2,128,256]{2,1,0:T(8,128)} %slice.685), channel_id=1, source_target_pairs={{1,0},{2,1},{3,2},{4,3},{5,4},{6,5},{7,6},{9,8},{10,9},{11,10},{12... | collective-permute-start | bytes 786440 | tf_op jit(solution)/shard_map/ppermute | solution.py:19
  301.3 6.8 %copy-start.29 = (f32[8,128,256]{2,1,0:T(8,128)}, f32[8,128,256]{2,1,0:T(8,128)S(1)}, u32[]{:S(2)}) copy-start(f32[8,128,256]{2,1,0:T(8,128)S(1)} %get-tuple-element.93) | copy-start | bytes 3145732
  301.3 6.8 %copy-start.10 = (f32[8,128,256]{2,1,0:T(8,128)}, f32[8,128,256]{2,1,0:T(8,128)S(1)}, u32[]{:S(2)}) copy-start(f32[8,128,256]{2,1,0:T(8,128)S(1)} %get-tuple-element.94) | copy-start | bytes 3145732
  302.2 16.5 %collective-permute-start.10 = (f32[2,128,256]{2,1,0:T(8,128)}, f32[2,128,256]{2,1,0:T(8,128)S(1)}, u32[]{:S(2)}, u32[]{:S(2)}) collective-permute-start(f32[2,128,256]{2,1,0:T(8,128)} %get-tuple-element.119), channel_id=1, source_target_pairs={{0,1},{1,2},{2,3},{3,4},{4,5},{5,6},{6,7},{8,9},{9,10},{10,11},{11... | collective-permute-start | bytes 786440 | tf_op jit(solution)/shard_map/ppermute | solution.py:17
  306.8 11.9 %collective-permute-start.11 = (f32[2,128,256]{2,1,0:T(8,128)}, f32[2,128,256]{2,1,0:T(8,128)}, u32[]{:S(2)}, u32[]{:S(2)}) collective-permute-start(f32[2,128,256]{2,1,0:T(8,128)} %get-tuple-element.120), channel_id=1, source_target_pairs={{1,0},{2,1},{3,2},{4,3},{5,4},{6,5},{7,6},{9,8},{10,9},{11,10},{12... | collective-permute-start | bytes 786440 | tf_op jit(solution)/shard_map/ppermute | solution.py:19
  318.7 6.1 copy-start.7
  334.2 17.5 %copy-start.19 = (f32[8,128,256]{2,1,0:T(8,128)S(1)}, f32[8,128,256]{2,1,0:T(8,128)}, u32[]{:S(2)}) copy-start(f32[8,128,256]{2,1,0:T(8,128)} %reshape.382) | copy-start | bytes 3145732
  334.2 25.2 %copy-start.14 = (f32[8,128,256]{2,1,0:T(8,128)S(1)}, f32[8,128,256]{2,1,0:T(8,128)}, u32[]{:S(2)}) copy-start(f32[8,128,256]{2,1,0:T(8,128)} %copy-done.13) | copy-start | bytes 3145732
  334.3 25.2 %copy-start.16 = (f32[8,128,256]{2,1,0:T(8,128)S(1)}, f32[8,128,256]{2,1,0:T(8,128)}, u32[]{:S(2)}) copy-start(f32[8,128,256]{2,1,0:T(8,128)} %copy-done.15) | copy-start | bytes 3145732
  334.3 25.2 %copy-start.18 = (f32[8,128,256]{2,1,0:T(8,128)S(1)}, f32[8,128,256]{2,1,0:T(8,128)}, u32[]{:S(2)}) copy-start(f32[8,128,256]{2,1,0:T(8,128)} %get-tuple-element.81) | copy-start | bytes 3145732
  344.1 15.3 %copy-start.11 = (f32[8,128,256]{2,1,0:T(8,128)S(1)}, f32[8,128,256]{2,1,0:T(8,128)}, u32[]{:S(2)}) copy-start(f32[8,128,256]{2,1,0:T(8,128)} %copy-done.10) | copy-start | bytes 3145732
  345.3 8.7 %collective-permute-start.14 = (f32[2,128,256]{2,1,0:T(8,128)S(1)}, f32[2,128,256]{2,1,0:T(8,128)S(1)}, u32[]{:S(2)}, u32[]{:S(2)}) collective-permute-start(f32[2,128,256]{2,1,0:T(8,128)S(1)} %get-tuple-element.117), channel_id=1, source_target_pairs={{0,1},{1,2},{2,3},{3,4},{4,5},{5,6},{6,7},{8,9},{9,10},{10,11},{11... | collective-permute-start | bytes 786440 | tf_op jit(solution)/shard_map/ppermute | solution.py:17
  350.2 9.3 %copy-start.4 = (f32[8,128,256]{2,1,0:T(8,128)S(1)}, f32[8,128,256]{2,1,0:T(8,128)}, u32[]{:S(2)}) copy-start(f32[8,128,256]{2,1,0:T(8,128)} %copy-done.2) | copy-start | bytes 3145732
  350.2 9.3 %copy-start.6 = (f32[8,128,256]{2,1,0:T(8,128)S(1)}, f32[8,128,256]{2,1,0:T(8,128)}, u32[]{:S(2)}) copy-start(f32[8,128,256]{2,1,0:T(8,128)} %copy-done.5) | copy-start | bytes 3145732
  350.2 9.3 %copy-start.8 = (f32[8,128,256]{2,1,0:T(8,128)S(1)}, f32[8,128,256]{2,1,0:T(8,128)}, u32[]{:S(2)}) copy-start(f32[8,128,256]{2,1,0:T(8,128)} %reshape.378) | copy-start | bytes 3145732
  350.2 9.2 %collective-permute-start.15 = (f32[2,128,256]{2,1,0:T(8,128)S(1)}, f32[2,128,256]{2,1,0:T(8,128)S(1)}, u32[]{:S(2)}, u32[]{:S(2)}) collective-permute-start(f32[2,128,256]{2,1,0:T(8,128)S(1)} %get-tuple-element.118), channel_id=1, source_target_pairs={{1,0},{2,1},{3,2},{4,3},{5,4},{6,5},{7,6},{9,8},{10,9},{11,10},{12... | collective-permute-start | bytes 786440 | tf_op jit(solution)/shard_map/ppermute | solution.py:19
  (6 other events, 6.3 us)
Sparse Core Ops, SparseCore 0:
  11.3 81.8 all-gather.2
  96.6 74.6 all-gather.4
  367.5 277.7 all-reduce.18
where the time goes:
time: 664 us; the launch traced here: 654 us
  waiting for transfers between devices  446 us (67%)
  other arithmetic  82.2 us (12%)
  local copies, waits for them, and re-layouts  65.1 us (10%)
  starting transfers between devices  43.1 us (6%)
  between operations  17.1 us (3%)
    psum x1, waiting for transfers between devices, sum_shots(): whole_one, whole_two = lax.psum((first_term, second_term), 'shot')  278 us
    all_gather x1, waiting for transfers between devices, on_device(): lax.all_gather(epsilon, 'shot', axis=1, tiled=True)  78.1 us
    all_gather x1, waiting for transfers between devices, on_device(): lax.all_gather(velocity, 'shot', axis=1, tiled=True)  65.5 us
    ppermute x8, starting transfers between devices, with_halo(): lax.ppermute(tail, axis, [(i, (i + 1) % count) for i in range(ends)])  32.4 us
    unnamed x85, local copies, waits for them, and re-layouts  26.9 us
    ppermute x8, waiting for transfers between devices, with_halo(): lax.ppermute(head, axis, [((i + 1) % count, i) for i in range(ends)])  24.6 us
    scatter-add x10, other arithmetic, inject(): flattened = field.reshape(-1).at[layer_ids * plane_size + within].add(jnp...  19.4 us
    reshape x10, local copies, waits for them, and re-layouts, inject(): return flattened.reshape(field.shape)  17.5 us
  transfers between devices with their start and end apart: 19, of which 8 were waited for; matrix products, arithmetic and copies ran while one was open for 16% of the time, Pallas kernels for 0%

commit v1 on v0

--- a/solution.py
+++ b/solution.py
@@ -64,7 +64,9 @@
     velocity, epsilon, forward_state, adjoint_state, source_cell, wavelet, receiver_cells, residuals
 ):
     vel_slab, eps_slab = (
-        lax.all_gather(velocity, "shot", axis=1, tiled=True),
+        jnp.concatenate(
+            lax.all_to_all(jnp.stack([velocity] * lax.axis_size("shot")), "shot", 0, 0), axis=1
+        ),
         lax.all_gather(epsilon, "shot", axis=1, tiled=True),
     )
     stiffness = vel_slab * vel_slab

time: 664 us -> 637 us (0.959)
  waiting for transfers between devices: 446 us -> 348 us
  local copies, waits for them, and re-layouts: 65.1 us -> 101 us
  other arithmetic: 82.2 us -> 105 us
  starting transfers between devices: 43.1 us -> 56 us
    all_gather x1 -> x0, waiting for transfers between devices: 65.5 us -> none  [on_device(): lax.all_gather(velocity, 'shot', axis=1, tiled=True)]
    all_gather x1, waiting for transfers between devices: 78.1 us -> 52.8 us  [on_device(): lax.all_gather(epsilon, 'shot', axis=1, tiled=True)]
    ppermute x8, waiting for transfers between devices: 24.6 us -> 6.15 us  [with_halo(): lax.ppermute(head, axis, [((i + 1) % count, i) for i in range(ends)])]
    all_to_all x0 -> x1, starting transfers between devices: none -> 12.8 us  [on_device(): lax.all_to_all(jnp.stack([velocity] * lax.axis_size('shot')), 'shot', 0, 0)]
    reshape x10 -> x14, local copies, waits for them, and re-layouts: 17.5 us -> 29.8 us  [inject(): return flattened.reshape(field.shape)]
    all_to_all x0 -> x1, waiting for transfers between devices: none -> 9.13 us  [on_device(): lax.all_to_all(jnp.stack([velocity] * lax.axis_size('shot')), 'shot', 0, 0)]
    add x2, other arithmetic: 9.43 us -> 17.6 us  [on_device(): 2.0 * pressure_now - pressure_old]
    mul x3, other arithmetic: 12 us -> 19.5 us  [on_device(): stiffness * (stretch * back_now + side_now)]
  transfers between devices with their start and end apart: 19 -> 19, of which waited for: 8 -> 5; matrix products, arithmetic and copies ran while one was open for 16% -> 19% of each run, Pallas kernels for 0% -> 0%
where the time goes in v1:
time: 637 us; the launch traced here: 628 us
  waiting for transfers between devices  348 us (55%)
  other arithmetic  105 us (16%)
  local copies, waits for them, and re-layouts  101 us (16%)
  starting transfers between devices  56 us (9%)
  between operations  17.9 us (3%)
    psum x1, waiting for transfers between devices, sum_shots(): whole_one, whole_two = lax.psum((first_term, second_term), 'shot')  280 us
    all_gather x1, waiting for transfers between devices, on_device(): lax.all_gather(epsilon, 'shot', axis=1, tiled=True)  52.8 us
    ppermute x8, starting transfers between devices, with_halo(): lax.ppermute(tail, axis, [(i, (i + 1) % count) for i in range(ends)])  32.6 us
    reshape x14, local copies, waits for them, and re-layouts, inject(): return flattened.reshape(field.shape)  29.8 us
    unnamed x129, local copies, waits for them, and re-layouts  25.1 us
    scatter-add x10, other arithmetic, inject(): flattened = field.reshape(-1).at[layer_ids * plane_size + within].add(jnp...  24.8 us
    mul x3, other arithmetic, on_device(): stiffness * (stretch * back_now + side_now)  19.5 us
    add x2, other arithmetic, on_device(): 2.0 * pressure_now - pressure_old  17.6 us
  transfers between devices with their start and end apart: 19, of which 5 were waited for; matrix products, arithmetic and copies ran while one was open for 19% of the time, Pallas kernels for 0%

profile of v1, /device:TPU:1, one launch (start us, length us, event | category | flops | bytes accessed | tf_op | source)
XLA Modules:
  0.0 627.6 jit_solution(7487037487310886868)
XLA Ops:
  7.2 2.0 stack.2
  9.2 12.8 %all-to-all-start = ((f32[32,8,4,256]{3,2,1,0:T(4,128)}), f32[32,8,4,256]{3,2,1,0:T(4,128)}, u32[]{:S(2)}, u32[]{:S(2)}) async-start(f32[32,8,4,256]{3,2,1,0:T(4,128)} %stack.2), calls=%async_computation | async-start | bytes 2097152 | tf_op jit(solution)/shard_map/all_to_all | solution.py:68
  24.7 2.2 collective-permute-start
  31.8 3.9 fusion.171
  35.7 2.6 copy_bitcast_fusion.2
  39.0 2.1 fusion.173
  41.1 9.1 %all-to-all-done = f32[32,8,4,256]{3,2,1,0:T(4,128)} async-done(((f32[32,8,4,256]{3,2,1,0:T(4,128)}), f32[32,8,4,256]{3,2,1,0:T(4,128)}, u32[]{:S(2)}, u32[]{:S(2)}) %all-to-all-start) | async-done | bytes 1048608 | tf_op jit(solution)/shard_map/all_to_all | solution.py:68
  50.2 2.5 copy_multiply_fusion.1
  52.8 52.8 %all-gather.2.cloned.1.call-done = f32[8,128,256]{2,0,1:T(8,128)} async-done(((f32[8,4,256]{2,0,1:T(8,128)}), f32[8,128,256]{2,0,1:T(8,128)}) %all-gather.2.cloned.1.call-update) | async-done | bytes 1048592 | tf_op jit(solution)/shard_map/all_gather | solution.py:70
  105.6 11.3 %fusion.130 = (f32[8,128,256]{2,0,1:T(8,128)}, f32[8,128,256]{2,0,1:T(8,128)S(1)}, f32[8,128,256]{2,0,1:T(8,128)S(1)}) fusion(f32[1,1,8,128,256]{4,3,2,1,0:T(8,128)} %get-tuple-element.101, f32[32,8,4,256]{3,1,2,0:T(8,128)S(1)} %get-tuple-element.126, f32[8,128,256]{2,0,1:T(8,128)} %all-gather.2.cloned.1.call-done, ...), kind=kLoop, calls=%fused_computation.212 | loop fusion | flops 8650752 | bytes 9961472 | tf_op jit(solution)/shard_map/add | solution.py:103
  123.2 2.3 fusion.177
  130.7 4.2 collective-permute-start.2
  134.9 2.0 constant_dynamic-update-slice_fusion.1
  140.4 2.6 reshape.371
  143.0 2.0 copy.37
  146.8 6.3 %fusion.132 = (f32[8,128,256]{2,0,1:T(8,128)}, f32[8,128,256]{2,0,1:T(8,128)S(1)}, f32[8,128,256]{2,0,1:T(8,128)S(1)}) fusion(f32[32,8,4,256]{3,1,2,0:T(8,128)S(1)} %get-tuple-element.126, f32[8,128,256]{2,0,1:T(8,128)S(1)} %copy-done, f32[1,1,8,128,256]{4,3,2,1,0:T(8,128)S(1)} %get-tuple-element.102, f32[8,128,256]{2,1,0:T(8,128)S(1)} %copy-done.14, ...), kind=kLoop, calls=%fused_computation.233 | loop fusion | flops 8126464 | bytes 11796480 | tf_op jit(solution)/shard_map/add | solution.py:103
  159.4 2.3 fusion.176
  166.9 4.4 collective-permute-start.4
  171.3 2.0 constant_dynamic-update-slice_fusion.3
  176.7 2.6 reshape.376
  179.3 2.0 copy.49
  181.3 1.8 constant_dynamic-update-slice_fusion.2
  183.1 6.5 %fusion.135 = (f32[8,128,256]{2,0,1:T(8,128)}, f32[8,128,256]{2,0,1:T(8,128)S(1)}, f32[8,128,256]{2,0,1:T(8,128)S(1)}) fusion(f32[32,8,4,256]{3,1,2,0:T(8,128)S(1)} %get-tuple-element.126, f32[8,128,256]{2,1,0:T(8,128)S(1)} %copy-done.33, f32[8,128,256]{2,1,0:T(8,128)S(1)} %copy-done.18, f32[8,128,256]{2,0,1:T(8,128)S(1)} %copy.49, ...), kind=kLoop, calls=%fused_computation.236 | loop fusion | flops 7340032 | bytes 10747904 | tf_op jit(solution)/shard_map/add | solution.py:105
  189.7 3.6 bitcast_multiply_fusion.8
  194.4 4.0 collective-permute-start.6
  203.2 4.3 scatter_fusion
  209.6 6.5 %bitcast_multiply_fusion.7 = (f32[8,128,256]{2,0,1:T(8,128)S(1)}, f32[8,128,256]{2,0,1:T(8,128)S(1)}) fusion(f32[32,8,4,256]{3,1,2,0:T(8,128)S(1)} %get-tuple-element.126, f32[8,128,256]{2,1,0:T(8,128)S(1)} %reshape.367, f32[8,128,256]{2,0,1:T(8,128)S(1)} %copy-done, f32[8,128,256]{2,0,1:T(8,128)} %copy-done.41, f32[2,128,256]{2,0,1:T(2,128)} %collective-permute-done.7, ...), kind=kLoop, calls=%fused_computation.225 | loop fusion | flops 4980736 | bytes 8912896 | tf_op jit(solution)/shard_map/mul | solution.py:115
  216.1 2.8 bitcast_multiply_fusion.6
  220.8 4.0 collective-permute-start.8
  231.0 4.3 scatter_fusion.1
  235.3 2.5 reshape.383
  237.8 6.2 bitcast_multiply_fusion.5
  244.1 2.8 bitcast_multiply_fusion.4
  248.9 4.7 collective-permute-start.10
  255.7 2.5 reshape.389
  266.1 2.5 reshape.381
  268.6 2.8 copy.62
  273.4 4.6 collective-permute-start.12
  281.1 4.4 scatter_fusion.2
  285.5 2.5 reshape.385
  288.0 6.8 %bitcast_multiply_fusion.3 = (f32[8,128,256]{2,0,1:T(8,128)S(1)}, f32[8,128,256]{2,0,1:T(8,128)}) fusion(f32[32,8,4,256]{3,1,2,0:T(8,128)S(1)} %get-tuple-element.126, f32[8,128,256]{2,1,0:T(8,128)} %reshape.385, f32[8,128,256]{2,0,1:T(8,128)S(1)} %copy-done, f32[8,128,256]{2,0,1:T(8,128)} %copy-done.39, f32[2,128,256]{2,0,1:T(2,128)} %collective-permute-done.11, ...), kind=kLoop, calls=%fused_computation.221 | loop fusion | flops 4980736 | bytes 8912896 | tf_op jit(solution)/shard_map/mul | solution.py:115
  298.2 4.1 scatter_fusion.3
  302.3 2.5 reshape.387
  304.9 12.3 %fusion.136 = (f32[8,128,256]{2,0,1:T(8,128)}, f32[8,128,256]{2,0,1:T(8,128)S(1)}, f32[8,128,256]{2,0,1:T(8,128)S(1)}) fusion(f32[32,8,4,256]{3,1,2,0:T(8,128)S(1)} %get-tuple-element.126, f32[8,128,256]{2,0,1:T(8,128)} %copy-done.10, f32[8,128,256]{2,1,0:T(8,128)} %reshape.387, f32[8,128,256]{2,0,1:T(8,128)} %copy-done.12, f32[8,128,256]{2,1,0:T(8,128)} %reshape.385, ...), kind=kLoop, calls=%fused_computation.237 | loop fusion | flops 6553600 | bytes 13631488 | tf_op jit(solution)/shard_map/mul | solution.py:128
  317.4 4.5 collective-permute-start.14
  325.3 5.6 collective-permute-done.15
  330.9 6.6 %fusion.69 = f32[8,128,256]{2,0,1:T(8,128)} fusion(f32[8,128,256]{2,0,1:T(8,128)S(1)} %get-tuple-element.112, f32[2,128,256]{2,0,1:T(2,128)S(1)} %collective-permute-done.15, f32[2,128,256]{2,0,1:T(2,128)S(1)} %collective-permute-done.14, f32[32,8,4,256]{3,1,2,0:T(8,128)S(1)} %copy-done.42, f32[8,128,256]{2,0,1:T(8,128)S(1)} %copy-done.9, ...), kind=kLoop, calls=%fused_computation.131 | loop fusion | flops 14155776 | bytes 22806528 | tf_op jit(solution)/shard_map/mul | solution.py:127
  337.6 279.9 %all-reduce.19.cloned.1.call-done = (f32[8,128,256]{2,0,1:T(8,128)}, f32[8,128,256]{2,0,1:T(8,128)}) async-done(((f32[8,128,256]{2,0,1:T(8,128)}, f32[8,128,256]{2,0,1:T(8,128)}), (f32[8,128,256]{2,0,1:T(8,128)}, f32[8,128,256]{2,0,1:T(8,128)})) %all-reduce.19.cloned.1.call-update) | async-done | bytes 2097168 | tf_op jit(solution)/shard_map/psum | solution.py:55
  (205 shorter events, 80.2 us)
Async XLA Ops:
  7.2 14.8 %copy-start.52 = (f32[8,4,256]{2,1,0:T(4,128)S(1)}, f32[8,4,256]{2,1,0:T(4,128)}, u32[]{:S(2)}) copy-start(f32[8,4,256]{2,1,0:T(4,128)} %param.21) | copy-start | bytes 98308
  9.2 20.0 %copy-start.55 = (s32[1,256]{1,0:T(1,128)S(1)}, s32[1,256]{1,0:T(1,128)}, u32[]{:S(2)}) copy-start(s32[1,256]{1,0:T(1,128)} %param.26) | copy-start | bytes 3076
  9.2 20.0 %copy-start.53 = (f32[1,3]{1,0:T(1,128)S(1)}, f32[1,3]{1,0:T(1,128)}, u32[]{:S(2)}) copy-start(f32[1,3]{1,0:T(1,128)} %param.25) | copy-start | bytes 40
  9.2 22.5 %copy-start.54 = (f32[1,4,256]{2,1,0:T(4,128)S(1)}, f32[1,4,256]{2,1,0:T(4,128)}, u32[]{:S(2)}) copy-start(f32[1,4,256]{2,1,0:T(4,128)} %param.27) | copy-start | bytes 12292
  9.2 41.1 %all-to-all-start = ((f32[32,8,4,256]{3,2,1,0:T(4,128)}), f32[32,8,4,256]{3,2,1,0:T(4,128)}, u32[]{:S(2)}, u32[]{:S(2)}) async-start(f32[32,8,4,256]{3,2,1,0:T(4,128)} %stack.2), calls=%async_computation | async-start | bytes 2097152 | tf_op jit(solution)/shard_map/all_to_all | solution.py:68
  21.9 83.6 %all-gather.2.cloned.1.call-start = ((), (), s32[]{:S(2)}) async-start(), calls=%async_computation.1 | async-start | bytes 1081344 | tf_op jit(solution)/shard_map/all_gather | solution.py:70
  22.7 594.8 %all-reduce.19.cloned.1.call-start = ((), (), s32[]{:S(2)}) async-start(), calls=%async_computation.2 | async-start | bytes 4194304 | tf_op jit(solution)/shard_map/psum | solution.py:55
  24.7 28.1 %collective-permute-start = (f32[2,128,256]{2,0,1:T(2,128)}, f32[2,128,256]{2,0,1:T(2,128)S(1)}, u32[]{:S(2)}, u32[]{:S(2)}) collective-permute-start(f32[2,128,256]{2,0,1:T(2,128)} %bitcast.149), channel_id=1, source_target_pairs={{0,1},{1,2},{2,3},{3,4},{4,5},{5,6},{6,7},{8,9},{9,10},{10,11},{11... | collective-permute-start | bytes 786440 | tf_op jit(solution)/shard_map/ppermute | solution.py:17
  27.8 24.9 %collective-permute-start.1 = (f32[2,128,256]{2,0,1:T(2,128)}, f32[2,128,256]{2,0,1:T(2,128)}, u32[]{:S(2)}, u32[]{:S(2)}) collective-permute-start(f32[2,128,256]{2,0,1:T(2,128)} %bitcast.148), channel_id=1, source_target_pairs={{1,0},{2,1},{3,2},{4,3},{5,4},{6,5},{7,6},{9,8},{10,9},{11,10},{12... | collective-permute-start | bytes 786440 | tf_op jit(solution)/shard_map/ppermute | solution.py:19
  35.7 81.2 %copy-start.22 = (f32[1,1,8,128,256]{4,3,2,1,0:T(8,128)}, f32[1,1,8,128,256]{4,3,2,1,0:T(8,128)S(1)}, u32[]{:S(2)}) copy-start(f32[1,1,8,128,256]{4,3,2,1,0:T(8,128)S(1)} %get-tuple-element.100) | copy-start | bytes 3145732
  105.6 11.3 %copy-start.51 = (f32[1,1,8,128,256]{4,3,2,1,0:T(8,128)S(1)}, f32[1,1,8,128,256]{4,3,2,1,0:T(8,128)}, u32[]{:S(2)}) copy-start(f32[1,1,8,128,256]{4,3,2,1,0:T(8,128)} %get-tuple-element.99) | copy-start | bytes 3145732
  123.2 13.7 %copy-start.16 = (f32[8,128,256]{2,1,0:T(8,128)}, f32[8,128,256]{2,1,0:T(8,128)S(1)}, u32[]{:S(2)}) copy-start(f32[8,128,256]{2,1,0:T(8,128)S(1)} %reshape.373) | copy-start | bytes 3145732
  127.5 17.5 %collective-permute-start.3 = (f32[2,128,256]{2,0,1:T(2,128)}, f32[2,128,256]{2,0,1:T(2,128)}, u32[]{:S(2)}, u32[]{:S(2)}) collective-permute-start(f32[2,128,256]{2,0,1:T(2,128)} %copy.45), channel_id=1, source_target_pairs={{1,0},{2,1},{3,2},{4,3},{5,4},{6,5},{7,6},{9,8},{10,9},{11,10},{12... | collective-permute-start | bytes 786440 | tf_op jit(solution)/shard_map/ppermute | solution.py:19
  129.8 7.1 %copy-start.45 = (f32[8,128,256]{2,0,1:T(8,128)S(1)}, f32[8,128,256]{2,0,1:T(8,128)}, u32[]{:S(2)}) copy-start(f32[8,128,256]{2,0,1:T(8,128)} %get-tuple-element.92) | copy-start | bytes 3145732
  130.7 16.1 %collective-permute-start.2 = (f32[2,128,256]{2,0,1:T(2,128)}, f32[2,128,256]{2,0,1:T(2,128)S(1)}, u32[]{:S(2)}, u32[]{:S(2)}) collective-permute-start(f32[2,128,256]{2,0,1:T(2,128)} %copy.43), channel_id=1, source_target_pairs={{0,1},{1,2},{2,3},{3,4},{4,5},{5,6},{6,7},{8,9},{9,10},{10,11},{11... | collective-permute-start | bytes 786440 | tf_op jit(solution)/shard_map/ppermute | solution.py:17
  159.4 13.9 %copy-start.32 = (f32[8,128,256]{2,1,0:T(8,128)}, f32[8,128,256]{2,1,0:T(8,128)S(1)}, u32[]{:S(2)}) copy-start(f32[8,128,256]{2,1,0:T(8,128)S(1)} %reshape.378) | copy-start | bytes 3145732
  163.7 17.6 %collective-permute-start.5 = (f32[2,128,256]{2,0,1:T(2,128)}, f32[2,128,256]{2,0,1:T(2,128)}, u32[]{:S(2)}, u32[]{:S(2)}) collective-permute-start(f32[2,128,256]{2,0,1:T(2,128)} %copy.58), channel_id=1, source_target_pairs={{1,0},{2,1},{3,2},{4,3},{5,4},{6,5},{7,6},{9,8},{10,9},{11,10},{12... | collective-permute-start | bytes 786440 | tf_op jit(solution)/shard_map/ppermute | solution.py:19
  166.0 7.4 %copy-start.46 = (f32[8,128,256]{2,0,1:T(8,128)S(1)}, f32[8,128,256]{2,0,1:T(8,128)}, u32[]{:S(2)}) copy-start(f32[8,128,256]{2,0,1:T(8,128)} %get-tuple-element.89) | copy-start | bytes 3145732
  166.9 16.2 %collective-permute-start.4 = (f32[2,128,256]{2,0,1:T(2,128)}, f32[2,128,256]{2,0,1:T(2,128)S(1)}, u32[]{:S(2)}, u32[]{:S(2)}) collective-permute-start(f32[2,128,256]{2,0,1:T(2,128)} %copy.56), channel_id=1, source_target_pairs={{0,1},{1,2},{2,3},{3,4},{4,5},{5,6},{6,7},{8,9},{9,10},{10,11},{11... | collective-permute-start | bytes 786440 | tf_op jit(solution)/shard_map/ppermute | solution.py:17
  189.7 10.1 %copy-start.50 = (f32[1,1,8,128,256]{4,3,2,1,0:T(8,128)S(1)}, f32[1,1,8,128,256]{4,3,2,1,0:T(8,128)}, u32[]{:S(2)}) copy-start(f32[1,1,8,128,256]{4,3,2,1,0:T(8,128)} %get-tuple-element.107) | copy-start | bytes 3145732
  193.3 8.0 %copy-start.41 = (f32[8,128,256]{2,0,1:T(8,128)}, f32[8,128,256]{2,0,1:T(8,128)S(1)}, u32[]{:S(2)}) copy-start(f32[8,128,256]{2,0,1:T(8,128)S(1)} %get-tuple-element.109) | copy-start | bytes 3145732
  194.4 14.6 %collective-permute-start.6 = (f32[2,128,256]{2,0,1:T(2,128)}, f32[2,128,256]{2,0,1:T(2,128)S(1)}, u32[]{:S(2)}, u32[]{:S(2)}) collective-permute-start(f32[2,128,256]{2,0,1:T(2,128)} %get-tuple-element.137), channel_id=1, source_target_pairs={{0,1},{1,2},{2,3},{3,4},{4,5},{5,6},{6,7},{8,9},{9,10},{10,11},{11... | collective-permute-start | bytes 786440 | tf_op jit(solution)/shard_map/ppermute | solution.py:17
  198.4 11.2 %collective-permute-start.7 = (f32[2,128,256]{2,0,1:T(2,128)}, f32[2,128,256]{2,0,1:T(2,128)}, u32[]{:S(2)}, u32[]{:S(2)}) collective-permute-start(f32[2,128,256]{2,0,1:T(2,128)} %get-tuple-element.138), channel_id=1, source_target_pairs={{1,0},{2,1},{3,2},{4,3},{5,4},{6,5},{7,6},{9,8},{10,9},{11,10},{12... | collective-permute-start | bytes 786440 | tf_op jit(solution)/shard_map/ppermute | solution.py:19
  220.8 17.0 %collective-permute-start.8 = (f32[2,128,256]{2,0,1:T(2,128)}, f32[2,128,256]{2,0,1:T(2,128)S(1)}, u32[]{:S(2)}, u32[]{:S(2)}) collective-permute-start(f32[2,128,256]{2,0,1:T(2,128)} %get-tuple-element.133), channel_id=1, source_target_pairs={{0,1},{1,2},{2,3},{3,4},{4,5},{5,6},{6,7},{8,9},{9,10},{10,11},{11... | collective-permute-start | bytes 786440 | tf_op jit(solution)/shard_map/ppermute | solution.py:17
  224.8 13.0 %collective-permute-start.9 = (f32[2,128,256]{2,0,1:T(2,128)}, f32[2,128,256]{2,0,1:T(2,128)}, u32[]{:S(2)}, u32[]{:S(2)}) collective-permute-start(f32[2,128,256]{2,0,1:T(2,128)} %get-tuple-element.134), channel_id=1, source_target_pairs={{1,0},{2,1},{3,2},{4,3},{5,4},{6,5},{7,6},{9,8},{10,9},{11,10},{12... | collective-permute-start | bytes 786440 | tf_op jit(solution)/shard_map/ppermute | solution.py:19
  244.1 10.7 %copy-start.38 = (f32[262144]{0:T(1024)S(1)}, f32[262144]{0:T(1024)}, u32[]{:S(2)}) copy-start(f32[262144]{0:T(1024)} %copy-done.37) | copy-start | bytes 3145732
  248.9 39.1 %collective-permute-start.10 = (f32[2,128,256]{2,0,1:T(2,128)}, f32[2,128,256]{2,0,1:T(2,128)}, u32[]{:S(2)}, u32[]{:S(2)}) collective-permute-start(f32[2,128,256]{2,0,1:T(2,128)} %get-tuple-element.129), channel_id=1, source_target_pairs={{0,1},{1,2},{2,3},{3,4},{4,5},{5,6},{6,7},{8,9},{9,10},{10,11},{11... | collective-permute-start | bytes 786440 | tf_op jit(solution)/shard_map/ppermute | solution.py:17
  253.6 34.5 %collective-permute-start.11 = (f32[2,128,256]{2,0,1:T(2,128)}, f32[2,128,256]{2,0,1:T(2,128)}, u32[]{:S(2)}, u32[]{:S(2)}) collective-permute-start(f32[2,128,256]{2,0,1:T(2,128)} %get-tuple-element.130), channel_id=1, source_target_pairs={{1,0},{2,1},{3,2},{4,3},{5,4},{6,5},{7,6},{9,8},{10,9},{11,10},{12... | collective-permute-start | bytes 786440 | tf_op jit(solution)/shard_map/ppermute | solution.py:19
  260.2 64.0 %collective-permute-start.13 = (f32[2,128,256]{2,0,1:T(2,128)}, f32[2,128,256]{2,0,1:T(2,128)}, u32[]{:S(2)}, u32[]{:S(2)}) collective-permute-start(f32[2,128,256]{2,0,1:T(2,128)} %copy.88), channel_id=1, source_target_pairs={{1,0},{2,1},{3,2},{4,3},{5,4},{6,5},{7,6},{9,8},{10,9},{11,10},{12... | collective-permute-start | bytes 786440 | tf_op jit(solution)/shard_map/ppermute | solution.py:19
  273.4 51.9 %collective-permute-start.12 = (f32[2,128,256]{2,0,1:T(2,128)}, f32[2,128,256]{2,0,1:T(2,128)S(1)}, u32[]{:S(2)}, u32[]{:S(2)}) collective-permute-start(f32[2,128,256]{2,0,1:T(2,128)} %copy.86), channel_id=1, source_target_pairs={{0,1},{1,2},{2,3},{3,4},{4,5},{5,6},{6,7},{8,9},{9,10},{10,11},{11... | collective-permute-start | bytes 786440 | tf_op jit(solution)/shard_map/ppermute | solution.py:17
  288.0 6.8 %copy-start.2 = (f32[8,128,256]{2,1,0:T(8,128)S(1)}, f32[8,128,256]{2,1,0:T(8,128)}, u32[]{:S(2)}) copy-start(f32[8,128,256]{2,1,0:T(8,128)} %reshape.383) | copy-start | bytes 3145732
  288.0 6.8 %copy-start.6 = (f32[8,128,256]{2,1,0:T(8,128)S(1)}, f32[8,128,256]{2,1,0:T(8,128)}, u32[]{:S(2)}) copy-start(f32[8,128,256]{2,1,0:T(8,128)} %reshape.385) | copy-start | bytes 3145732
  304.8 18.7 %copy-start.44 = (f32[8,128,256]{2,1,0:T(8,128)S(1)}, f32[8,128,256]{2,1,0:T(8,128)}, u32[]{:S(2)}) copy-start(f32[8,128,256]{2,1,0:T(8,128)} %reshape.389) | copy-start | bytes 3145732
  304.8 26.0 %copy-start.11 = (f32[8,128,256]{2,0,1:T(8,128)S(1)}, f32[8,128,256]{2,0,1:T(8,128)}, u32[]{:S(2)}) copy-start(f32[8,128,256]{2,0,1:T(8,128)} %copy-done.10) | copy-start | bytes 3145732
  304.8 26.0 %copy-start.13 = (f32[8,128,256]{2,0,1:T(8,128)S(1)}, f32[8,128,256]{2,0,1:T(8,128)}, u32[]{:S(2)}) copy-start(f32[8,128,256]{2,0,1:T(8,128)} %copy-done.12) | copy-start | bytes 3145732
  304.8 26.0 %copy-start.25 = (f32[8,128,256]{2,0,1:T(8,128)S(1)}, f32[8,128,256]{2,0,1:T(8,128)}, u32[]{:S(2)}) copy-start(f32[8,128,256]{2,0,1:T(8,128)} %copy-done.24) | copy-start | bytes 3145732
  304.9 26.0 %copy-start.27 = (f32[8,128,256]{2,0,1:T(8,128)S(1)}, f32[8,128,256]{2,0,1:T(8,128)}, u32[]{:S(2)}) copy-start(f32[8,128,256]{2,0,1:T(8,128)} %copy-done.26) | copy-start | bytes 3145732
  304.9 26.0 %copy-start.29 = (f32[8,128,256]{2,0,1:T(8,128)S(1)}, f32[8,128,256]{2,0,1:T(8,128)}, u32[]{:S(2)}) copy-start(f32[8,128,256]{2,0,1:T(8,128)} %copy-done.28) | copy-start | bytes 3145732
  304.9 26.0 %copy-start.30 = (f32[8,128,256]{2,0,1:T(8,128)S(1)}, f32[8,128,256]{2,0,1:T(8,128)}, u32[]{:S(2)}) copy-start(f32[8,128,256]{2,0,1:T(8,128)} %get-tuple-element.85) | copy-start | bytes 3145732
  304.9 26.0 %copy-start.31 = (f32[8,128,256]{2,1,0:T(8,128)S(1)}, f32[8,128,256]{2,1,0:T(8,128)}, u32[]{:S(2)}) copy-start(f32[8,128,256]{2,1,0:T(8,128)} %reshape.387) | copy-start | bytes 3145732
  304.9 26.0 %copy-start.36 = (f32[8,128,256]{2,0,1:T(8,128)S(1)}, f32[8,128,256]{2,0,1:T(8,128)}, u32[]{:S(2)}) copy-start(f32[8,128,256]{2,0,1:T(8,128)} %copy-done.35) | copy-start | bytes 3145732
  304.9 26.0 %copy-start.42 = (f32[32,8,4,256]{3,1,2,0:T(8,128)S(1)}, f32[32,8,4,256]{3,1,2,0:T(8,128)}, u32[]{:S(2)}) copy-start(f32[32,8,4,256]{3,1,2,0:T(8,128)} %get-tuple-element.125) | copy-start | bytes 3145732
  317.2 13.7 %copy-start.9 = (f32[8,128,256]{2,0,1:T(8,128)S(1)}, f32[8,128,256]{2,0,1:T(8,128)}, u32[]{:S(2)}) copy-start(f32[8,128,256]{2,0,1:T(8,128)} %copy-done.8) | copy-start | bytes 3145732
  317.4 13.5 %copy-start.3 = (f32[8,128,256]{2,1,0:T(8,128)S(1)}, f32[8,128,256]{2,1,0:T(8,128)}, u32[]{:S(2)}) copy-start(f32[8,128,256]{2,1,0:T(8,128)} %reshape.383) | copy-start | bytes 3145732
  317.4 13.5 %copy-start.5 = (f32[8,128,256]{2,0,1:T(8,128)S(1)}, f32[8,128,256]{2,0,1:T(8,128)}, u32[]{:S(2)}) copy-start(f32[8,128,256]{2,0,1:T(8,128)} %copy-done.4) | copy-start | bytes 3145732
  317.4 13.5 %copy-start.7 = (f32[8,128,256]{2,1,0:T(8,128)S(1)}, f32[8,128,256]{2,1,0:T(8,128)}, u32[]{:S(2)}) copy-start(f32[8,128,256]{2,1,0:T(8,128)} %reshape.385) | copy-start | bytes 3145732
  317.4 7.8 %collective-permute-start.14 = (f32[2,128,256]{2,0,1:T(2,128)S(1)}, f32[2,128,256]{2,0,1:T(2,128)S(1)}, u32[]{:S(2)}, u32[]{:S(2)}) collective-permute-start(f32[2,128,256]{2,0,1:T(2,128)S(1)} %get-tuple-element.127), channel_id=1, source_target_pairs={{0,1},{1,2},{2,3},{3,4},{4,5},{5,6},{6,7},{8,9},{9,10},{10,11},{11... | collective-permute-start | bytes 786440 | tf_op jit(solution)/shard_map/ppermute | solution.py:17
  321.9 8.9 %collective-permute-start.15 = (f32[2,128,256]{2,0,1:T(2,128)S(1)}, f32[2,128,256]{2,0,1:T(2,128)S(1)}, u32[]{:S(2)}, u32[]{:S(2)}) collective-permute-start(f32[2,128,256]{2,0,1:T(2,128)S(1)} %get-tuple-element.128), channel_id=1, source_target_pairs={{1,0},{2,1},{3,2},{4,3},{5,4},{6,5},{7,6},{9,8},{10,9},{11,10},{12... | collective-permute-start | bytes 786440 | tf_op jit(solution)/shard_map/ppermute | solution.py:19
  (27 other events, 107.8 us)
Sparse Core Ops, SparseCore 0:
  26.1 79.3 all-gather.1
  337.7 279.7 all-reduce.18
